TPU v7x, 128 devices: a whole 4x4x4 slice. The times are simulated.
128 devices in a mesh: section: 8 (over y_hi, z), seq: 16 (over x, y_lo, core).
Axes of the slice: x: 4, y: 4 (y_hi: 2, y_lo: 2; y = y_hi * 2 + y_lo), z: 4, core: 2. Of those that a mesh axis runs over, the one named last changes fastest.
Arguments:
- inbound_embedding_batches: bfloat16 [2, 128, 4096], replicated, may hold values from -16 to 16
- decoder_embedding_batches: bfloat16 [2, 128, 4096], replicated, may hold values from -16 to 16
- asking_projections: bfloat16 [8, 4096, 4096], P('section', None, 'seq'), may hold values from -0.09375 to 0.09375
- probe_projections: bfloat16 [8, 4096, 4096], P('section', None, 'seq'), may hold values from -0.09375 to 0.09375
- payload_projections: bfloat16 [8, 4096, 4096], P('section', None, 'seq'), may hold values from -0.09375 to 0.09375
- exit_projections: bfloat16 [8, 4096, 4096], P('section', 'seq'), may hold values from -0.1875 to 0.1875
- layer_rescale_weights: float32 [8, 4096], P('section'), may hold values from 0.1 to 1.9
- logit_sharpness: float32 [8, 64], P('section', 'seq'), may hold values from 0.5 to 3
- last_rescale_weights: float32 [4096], replicated, may hold values from 0.1 to 1.9
Outputs:
- section_out: bfloat16 [8, 2, 128, 4096], P('section')
All inputs are finite; a program needn't handle non-finite values.
Results may differ from a plain program's by a relative error of at most 0.025.
Values may be sent and summed in bfloat16 or wider, within the bound.
A program may use at most 64 MiB of HBM per device.

v0:
```python
import math
import jax
import jax.numpy as jnp
from jax import lax
from jax.sharding import PartitionSpec as P

epsilon = 1e-06


def from_behind(x, axis, by):
    count = lax.axis_size(axis)
    pairs = [(i, i + by) for i in range(count) if 0 <= i + by < count]
    return lax.ppermute(x, axis, pairs)


def broadcast(value, axis, source):
    kept = jnp.where(lax.axis_index(axis) == source, value, 0).astype(value.dtype)
    return lax.psum(kept, axis)


def normalize(row_block, gain_vector):
    values = row_block.astype(jnp.float32)
    factor = lax.rsqrt(jnp.mean(values * values, axis=-1, keepdims=True) + epsilon)
    return (values * factor * gain_vector).astype(jnp.bfloat16)


def unit_heads(projected):
    return (
        projected * lax.rsqrt(jnp.mean(projected * projected, axis=-1, keepdims=True) + epsilon)
    ).astype(jnp.bfloat16)


def attend(queries, keys_proj, values_proj, logit_divisor):
    length = queries.shape[0]
    key_length = keys_proj.shape[0]
    head_count = logit_divisor.shape[0]
    head_size = queries.shape[1] // head_count
    unit_query = unit_heads(queries.reshape(length, head_count, head_size))
    unit_key = unit_heads(keys_proj.reshape(key_length, head_count, head_size))
    values = values_proj.astype(jnp.bfloat16).reshape(key_length, head_count, head_size)
    scores = jnp.einsum("qhd,khd->hqk", unit_query, unit_key, preferred_element_type=jnp.float32)
    scores = scores * (logit_divisor[:, None, None] / math.sqrt(head_size))
    weights = jnp.exp(scores)
    weights = (weights / jnp.sum(weights, axis=-1, keepdims=True)).astype(jnp.bfloat16)
    blended_payloads = jnp.einsum(
        "hqk,khd->qhd", weights, values, preferred_element_type=jnp.float32
    )
    return blended_payloads.astype(jnp.bfloat16).reshape(length, head_count * head_size)


def shards(
    inbound_embedding_batches,
    decoder_embedding_batches,
    asking_projections,
    probe_projections,
    payload_projections,
    exit_projections,
    layer_rescale_weights,
    logit_sharpness,
    last_rescale_weights,
):
    section_count = lax.axis_size("section")
    seq_count = lax.axis_size("seq")
    present_layer_index = lax.axis_index("section")
    seq_index = lax.axis_index("seq")
    encoders = 3 * section_count // 8
    batches = inbound_embedding_batches.shape[0]
    length = inbound_embedding_batches.shape[1]
    width = inbound_embedding_batches.shape[2]
    share_rows = length // seq_count
    first_own = seq_index * share_rows
    ticks = section_count + batches - 1
    w_query = asking_projections[0]
    w_key = probe_projections[0]
    w_value = payload_projections[0]
    w_output = exit_projections[0]
    logit_divisor = logit_sharpness[0]
    gain_vector = layer_rescale_weights[0]
    is_encoder = present_layer_index < encoders

    def layer(stream, memory_raw):
        rescaled_activations = normalize(stream, gain_vector)
        remote = normalize(memory_raw, last_rescale_weights)
        source_kv = jnp.where(is_encoder, rescaled_activations, remote)
        queries = jnp.dot(rescaled_activations, w_query, preferred_element_type=jnp.float32)
        keys_proj = jnp.dot(source_kv, w_key, preferred_element_type=jnp.float32)
        values_proj = jnp.dot(source_kv, w_value, preferred_element_type=jnp.float32)
        blended_payloads = attend(queries, keys_proj, values_proj, logit_divisor)
        update = lax.psum_scatter(
            jnp.dot(blended_payloads, w_output, preferred_element_type=jnp.float32).astype(
                jnp.bfloat16
            ),
            "seq",
            scatter_dimension=0,
            tiled=True,
        ).astype(jnp.float32)
        own_rows = lax.dynamic_slice_in_dim(stream, first_own, share_rows, 0)
        return (own_rows.astype(jnp.float32) + update).astype(jnp.bfloat16)

    blank = jnp.zeros((length, width), inbound_embedding_batches.dtype)
    holder = jnp.zeros((batches,) + blank.shape, inbound_embedding_batches.dtype)

    def advance(tick_index, state_tuple):
        arrived, carried, stored, finished = state_tuple
        offset = tick_index - present_layer_index
        batch_index = jnp.clip(offset, 0, batches - 1)
        valid = (offset >= 0) & (offset < batches)
        source_rows = lax.dynamic_index_in_dim(
            inbound_embedding_batches, batch_index, 0, keepdims=False
        )
        target_rows = lax.dynamic_index_in_dim(
            decoder_embedding_batches, batch_index, 0, keepdims=False
        )
        memory_kept = lax.dynamic_index_in_dim(stored, batch_index, 0, keepdims=False)
        arrived_rows = arrived
        stream = jnp.where(
            present_layer_index == 0,
            source_rows,
            jnp.where(present_layer_index == encoders, target_rows, arrived_rows),
        )
        share = layer(stream, memory_kept)
        outgoing = lax.all_gather(share, "seq", axis=0, tiled=True)
        written = lax.dynamic_update_index_in_dim(finished, outgoing, batch_index, 0)
        finished = jnp.where(valid, written, finished)
        arrived = from_behind(outgoing, "section", 1)
        encoded = broadcast(outgoing, "section", encoders - 1)
        produced = tick_index - (encoders - 1)
        ready = (produced >= 0) & (produced < batches)
        placed = lax.dynamic_update_index_in_dim(
            stored, encoded, jnp.clip(produced, 0, batches - 1), 0
        )
        stored = jnp.where(ready, placed, stored)
        return (arrived, carried, stored, finished)

    final_state = lax.fori_loop(0, ticks, advance, (blank, blank, holder, holder))
    finished = final_state[3]
    return finished[None]


def solution(mesh):
    return jax.shard_map(
        shards,
        mesh=mesh,
        in_specs=(
            P(),
            P(),
            P("section", None, "seq"),
            P("section", None, "seq"),
            P("section", None, "seq"),
            P("section", "seq", None),
            P("section", None),
            P("section", "seq"),
            P(),
        ),
        out_specs=P("section", None, None, None),
        check_vma=False,
    )
```

profile of v0, /device:TPU:0, one launch (start us, length us, event | category | flops | bytes accessed | tf_op | source)
XLA Modules:
  0.0 1826.0 jit_solution(14866793786622618340)
XLA Ops:
  9.4 1809.7 %while.19 = (s32[]{:T(128)}, bf16[128,4096]{1,0:T(8,128)(2,1)}, bf16[2,128,4096]{2,1,0:T(8,128)(2,1)S(1)}, bf16[2,128,4096]{2,1,0:T(8,128)(2,1)}, pred[]{:T(512)...) while((s32[]{:T(128)}, bf16[128,4096]{1,0:T(8,128)(2,1)}, ...), condition=%wide.region_8.9_spmd, body=%wide.region_0.8_spmd.sunk | while | flops 1104807808 | bytes 77665632 | solution.py:135
  10.1 2.8 fusion.48
  21.4 3.0 convolution_convert_fusion.8
  24.5 65.1 %reduce-scatter.2.cloned.1.call-done = bf16[8,4096]{1,0:T(8,128)(2,1)} async-done(((bf16[128,4096]{1,0:T(8,128)(2,1)}), bf16[8,4096]{1,0:T(8,128)(2,1)}) %reduce-scatter.2.cloned.1.call-update) | async-done | bytes 65552 | tf_op jit(solution)/shard_map/while/body/eval_jaxpr/reduce_scatter | solution.py:89
  91.2 30.5 %all-gather.2.cloned.1.call-done = bf16[128,4096]{1,0:T(8,128)(2,1)} async-done(((bf16[8,4096]{1,0:T(8,128)(2,1)}), bf16[128,4096]{1,0:T(8,128)(2,1)}) %all-gather.2.cloned.1.call-update) | async-done | bytes 1048592 | tf_op jit(solution)/shard_map/while/body/eval_jaxpr/all_gather | solution.py:122
  123.3 4.4 collective-permute-start
  130.2 83.9 %all-reduce.2.cloned.1.call-done = bf16[1,128,4096]{2,1,0:T(8,128)(2,1)} async-done(((bf16[1,128,4096]{2,1,0:T(8,128)(2,1)}), bf16[1,128,4096]{2,1,0:T(8,128)(2,1)}) %all-reduce.2.cloned.1.call-update) | async-done | bytes 1048592 | tf_op jit(solution)/shard_map/while/body/eval_jaxpr/psum | solution.py:18
  215.0 2.8 fusion.48
  226.4 3.0 convolution_convert_fusion.8
  229.5 60.3 %reduce-scatter.2.cloned.1.call-done = bf16[8,4096]{1,0:T(8,128)(2,1)} async-done(((bf16[128,4096]{1,0:T(8,128)(2,1)}), bf16[8,4096]{1,0:T(8,128)(2,1)}) %reduce-scatter.2.cloned.1.call-update) | async-done | bytes 65552 | tf_op jit(solution)/shard_map/while/body/eval_jaxpr/reduce_scatter | solution.py:89
  291.3 30.7 %all-gather.2.cloned.1.call-done = bf16[128,4096]{1,0:T(8,128)(2,1)} async-done(((bf16[8,4096]{1,0:T(8,128)(2,1)}), bf16[128,4096]{1,0:T(8,128)(2,1)}) %all-gather.2.cloned.1.call-update) | async-done | bytes 1048592 | tf_op jit(solution)/shard_map/while/body/eval_jaxpr/all_gather | solution.py:122
  323.6 4.4 collective-permute-start
  330.5 83.7 %all-reduce.2.cloned.1.call-done = bf16[1,128,4096]{2,1,0:T(8,128)(2,1)} async-done(((bf16[1,128,4096]{2,1,0:T(8,128)(2,1)}), bf16[1,128,4096]{2,1,0:T(8,128)(2,1)}) %all-reduce.2.cloned.1.call-update) | async-done | bytes 1048592 | tf_op jit(solution)/shard_map/while/body/eval_jaxpr/psum | solution.py:18
  426.5 3.0 convolution_convert_fusion.8
  429.7 60.4 %reduce-scatter.2.cloned.1.call-done = bf16[8,4096]{1,0:T(8,128)(2,1)} async-done(((bf16[128,4096]{1,0:T(8,128)(2,1)}), bf16[8,4096]{1,0:T(8,128)(2,1)}) %reduce-scatter.2.cloned.1.call-update) | async-done | bytes 65552 | tf_op jit(solution)/shard_map/while/body/eval_jaxpr/reduce_scatter | solution.py:89
  491.6 30.7 %all-gather.2.cloned.1.call-done = bf16[128,4096]{1,0:T(8,128)(2,1)} async-done(((bf16[8,4096]{1,0:T(8,128)(2,1)}), bf16[128,4096]{1,0:T(8,128)(2,1)}) %all-gather.2.cloned.1.call-update) | async-done | bytes 1048592 | tf_op jit(solution)/shard_map/while/body/eval_jaxpr/all_gather | solution.py:122
  524.0 4.4 collective-permute-start
  530.8 83.8 %all-reduce.2.cloned.1.call-done = bf16[1,128,4096]{2,1,0:T(8,128)(2,1)} async-done(((bf16[1,128,4096]{2,1,0:T(8,128)(2,1)}), bf16[1,128,4096]{2,1,0:T(8,128)(2,1)}) %all-reduce.2.cloned.1.call-update) | async-done | bytes 1048592 | tf_op jit(solution)/shard_map/while/body/eval_jaxpr/psum | solution.py:18
  628.2 3.0 convolution_convert_fusion.8
  631.3 60.4 %reduce-scatter.2.cloned.1.call-done = bf16[8,4096]{1,0:T(8,128)(2,1)} async-done(((bf16[128,4096]{1,0:T(8,128)(2,1)}), bf16[8,4096]{1,0:T(8,128)(2,1)}) %reduce-scatter.2.cloned.1.call-update) | async-done | bytes 65552 | tf_op jit(solution)/shard_map/while/body/eval_jaxpr/reduce_scatter | solution.py:89
  693.3 30.8 %all-gather.2.cloned.1.call-done = bf16[128,4096]{1,0:T(8,128)(2,1)} async-done(((bf16[8,4096]{1,0:T(8,128)(2,1)}), bf16[128,4096]{1,0:T(8,128)(2,1)}) %all-gather.2.cloned.1.call-update) | async-done | bytes 1048592 | tf_op jit(solution)/shard_map/while/body/eval_jaxpr/all_gather | solution.py:122
  725.7 4.4 collective-permute-start
  732.5 83.7 %all-reduce.2.cloned.1.call-done = bf16[1,128,4096]{2,1,0:T(8,128)(2,1)} async-done(((bf16[1,128,4096]{2,1,0:T(8,128)(2,1)}), bf16[1,128,4096]{2,1,0:T(8,128)(2,1)}) %all-reduce.2.cloned.1.call-update) | async-done | bytes 1048592 | tf_op jit(solution)/shard_map/while/body/eval_jaxpr/psum | solution.py:18
  829.8 3.0 convolution_convert_fusion.8
  832.9 60.4 %reduce-scatter.2.cloned.1.call-done = bf16[8,4096]{1,0:T(8,128)(2,1)} async-done(((bf16[128,4096]{1,0:T(8,128)(2,1)}), bf16[8,4096]{1,0:T(8,128)(2,1)}) %reduce-scatter.2.cloned.1.call-update) | async-done | bytes 65552 | tf_op jit(solution)/shard_map/while/body/eval_jaxpr/reduce_scatter | solution.py:89
  894.9 30.5 %all-gather.2.cloned.1.call-done = bf16[128,4096]{1,0:T(8,128)(2,1)} async-done(((bf16[8,4096]{1,0:T(8,128)(2,1)}), bf16[128,4096]{1,0:T(8,128)(2,1)}) %all-gather.2.cloned.1.call-update) | async-done | bytes 1048592 | tf_op jit(solution)/shard_map/while/body/eval_jaxpr/all_gather | solution.py:122
  927.0 4.4 collective-permute-start
  933.9 83.7 %all-reduce.2.cloned.1.call-done = bf16[1,128,4096]{2,1,0:T(8,128)(2,1)} async-done(((bf16[1,128,4096]{2,1,0:T(8,128)(2,1)}), bf16[1,128,4096]{2,1,0:T(8,128)(2,1)}) %all-reduce.2.cloned.1.call-update) | async-done | bytes 1048592 | tf_op jit(solution)/shard_map/while/body/eval_jaxpr/psum | solution.py:18
  1029.9 3.0 convolution_convert_fusion.8
  1033.0 60.4 %reduce-scatter.2.cloned.1.call-done = bf16[8,4096]{1,0:T(8,128)(2,1)} async-done(((bf16[128,4096]{1,0:T(8,128)(2,1)}), bf16[8,4096]{1,0:T(8,128)(2,1)}) %reduce-scatter.2.cloned.1.call-update) | async-done | bytes 65552 | tf_op jit(solution)/shard_map/while/body/eval_jaxpr/reduce_scatter | solution.py:89
  1095.0 30.7 %all-gather.2.cloned.1.call-done = bf16[128,4096]{1,0:T(8,128)(2,1)} async-done(((bf16[8,4096]{1,0:T(8,128)(2,1)}), bf16[128,4096]{1,0:T(8,128)(2,1)}) %all-gather.2.cloned.1.call-update) | async-done | bytes 1048592 | tf_op jit(solution)/shard_map/while/body/eval_jaxpr/all_gather | solution.py:122
  1127.3 4.4 collective-permute-start
  1134.1 83.7 %all-reduce.2.cloned.1.call-done = bf16[1,128,4096]{2,1,0:T(8,128)(2,1)} async-done(((bf16[1,128,4096]{2,1,0:T(8,128)(2,1)}), bf16[1,128,4096]{2,1,0:T(8,128)(2,1)}) %all-reduce.2.cloned.1.call-update) | async-done | bytes 1048592 | tf_op jit(solution)/shard_map/while/body/eval_jaxpr/psum | solution.py:18
  1230.2 3.0 convolution_convert_fusion.8
  1233.3 60.4 %reduce-scatter.2.cloned.1.call-done = bf16[8,4096]{1,0:T(8,128)(2,1)} async-done(((bf16[128,4096]{1,0:T(8,128)(2,1)}), bf16[8,4096]{1,0:T(8,128)(2,1)}) %reduce-scatter.2.cloned.1.call-update) | async-done | bytes 65552 | tf_op jit(solution)/shard_map/while/body/eval_jaxpr/reduce_scatter | solution.py:89
  1295.3 30.7 %all-gather.2.cloned.1.call-done = bf16[128,4096]{1,0:T(8,128)(2,1)} async-done(((bf16[8,4096]{1,0:T(8,128)(2,1)}), bf16[128,4096]{1,0:T(8,128)(2,1)}) %all-gather.2.cloned.1.call-update) | async-done | bytes 1048592 | tf_op jit(solution)/shard_map/while/body/eval_jaxpr/all_gather | solution.py:122
  1327.6 4.4 collective-permute-start
  1334.4 83.8 %all-reduce.2.cloned.1.call-done = bf16[1,128,4096]{2,1,0:T(8,128)(2,1)} async-done(((bf16[1,128,4096]{2,1,0:T(8,128)(2,1)}), bf16[1,128,4096]{2,1,0:T(8,128)(2,1)}) %all-reduce.2.cloned.1.call-update) | async-done | bytes 1048592 | tf_op jit(solution)/shard_map/while/body/eval_jaxpr/psum | solution.py:18
  1430.5 3.0 convolution_convert_fusion.8
  1433.7 60.3 %reduce-scatter.2.cloned.1.call-done = bf16[8,4096]{1,0:T(8,128)(2,1)} async-done(((bf16[128,4096]{1,0:T(8,128)(2,1)}), bf16[8,4096]{1,0:T(8,128)(2,1)}) %reduce-scatter.2.cloned.1.call-update) | async-done | bytes 65552 | tf_op jit(solution)/shard_map/while/body/eval_jaxpr/reduce_scatter | solution.py:89
  1495.5 30.9 %all-gather.2.cloned.1.call-done = bf16[128,4096]{1,0:T(8,128)(2,1)} async-done(((bf16[8,4096]{1,0:T(8,128)(2,1)}), bf16[128,4096]{1,0:T(8,128)(2,1)}) %all-gather.2.cloned.1.call-update) | async-done | bytes 1048592 | tf_op jit(solution)/shard_map/while/body/eval_jaxpr/all_gather | solution.py:122
  1528.0 4.4 collective-permute-start
  1534.8 83.7 %all-reduce.2.cloned.1.call-done = bf16[1,128,4096]{2,1,0:T(8,128)(2,1)} async-done(((bf16[1,128,4096]{2,1,0:T(8,128)(2,1)}), bf16[1,128,4096]{2,1,0:T(8,128)(2,1)}) %all-reduce.2.cloned.1.call-update) | async-done | bytes 1048592 | tf_op jit(solution)/shard_map/while/body/eval_jaxpr/psum | solution.py:18
  1630.9 3.0 convolution_convert_fusion.8
  1634.0 60.4 %reduce-scatter.2.cloned.1.call-done = bf16[8,4096]{1,0:T(8,128)(2,1)} async-done(((bf16[128,4096]{1,0:T(8,128)(2,1)}), bf16[8,4096]{1,0:T(8,128)(2,1)}) %reduce-scatter.2.cloned.1.call-update) | async-done | bytes 65552 | tf_op jit(solution)/shard_map/while/body/eval_jaxpr/reduce_scatter | solution.py:89
  1696.0 30.6 %all-gather.2.cloned.1.call-done = bf16[128,4096]{1,0:T(8,128)(2,1)} async-done(((bf16[8,4096]{1,0:T(8,128)(2,1)}), bf16[128,4096]{1,0:T(8,128)(2,1)}) %all-gather.2.cloned.1.call-update) | async-done | bytes 1048592 | tf_op jit(solution)/shard_map/while/body/eval_jaxpr/all_gather | solution.py:122
  1728.2 4.4 collective-permute-start
  1735.1 83.7 %all-reduce.2.cloned.1.call-done = bf16[1,128,4096]{2,1,0:T(8,128)(2,1)} async-done(((bf16[1,128,4096]{2,1,0:T(8,128)(2,1)}), bf16[1,128,4096]{2,1,0:T(8,128)(2,1)}) %all-reduce.2.cloned.1.call-update) | async-done | bytes 1048592 | tf_op jit(solution)/shard_map/while/body/eval_jaxpr/psum | solution.py:18
  (331 shorter events, 160.1 us)
Async XLA Ops:
  9.5 80.2 %reduce-scatter.2.cloned.1.call-start = ((), (), s32[]{:S(2)}) async-start(), calls=%async_computation.1 | async-start | bytes 1114112 | tf_op jit(solution)/shard_map/while/body/eval_jaxpr/reduce_scatter | solution.py:89
  24.5 97.2 %all-gather.2.cloned.1.call-start = ((), (), s32[]{:S(2)}) async-start(), calls=%async_computation.2 | async-start | bytes 1114112 | tf_op jit(solution)/shard_map/while/body/eval_jaxpr/all_gather | solution.py:122
  91.1 122.9 %all-reduce.2.cloned.1.call-start = ((), (), s32[]{:S(2)}) async-start(), calls=%async_computation.3 | async-start | bytes 2097152 | tf_op jit(solution)/shard_map/while/body/eval_jaxpr/psum | solution.py:18
  123.3 91.1 %collective-permute-start = (bf16[128,4096]{1,0:T(8,128)(2,1)S(1)}, bf16[128,4096]{1,0:T(8,128)(2,1)}, u32[]{:S(2)}, u32[]{:S(2)}) collective-permute-start(bf16[128,4096]{1,0:T(8,128)(2,1)S(1)} %copy-done), channel_id=1, source_target_pairs={{0,16},{16,32},{32,48},{48,64},{64,80},{80,96},{96,112},{1,17},{17... | collective-permute-start | bytes 3145736 | tf_op jit(solution)/shard_map/while/body/eval_jaxpr/ppermute | solution.py:13
  130.2 84.2 %copy-start.5 = (f32[4096]{0:T(1024)S(1)}, f32[4096]{0:T(1024)}, u32[]{:S(2)}) copy-start(f32[4096]{0:T(1024)} %get-tuple-element.671) | copy-start | bytes 49156 | tf_op jit(solution)/shard_map/while
  130.2 84.2 %copy-start.8 = (f32[1,4]{1,0:T(1,128)S(1)}, f32[1,4]{1,0:T(1,128)}, u32[]{:S(2)}) copy-start(f32[1,4]{1,0:T(1,128)} %get-tuple-element.697) | copy-start | bytes 52 | tf_op jit(solution)/shard_map/while
  214.4 75.3 %reduce-scatter.2.cloned.1.call-start = ((), (), s32[]{:S(2)}) async-start(), calls=%async_computation.1 | async-start | bytes 1114112 | tf_op jit(solution)/shard_map/while/body/eval_jaxpr/reduce_scatter | solution.py:89
  229.4 92.6 %all-gather.2.cloned.1.call-start = ((), (), s32[]{:S(2)}) async-start(), calls=%async_computation.2 | async-start | bytes 1114112 | tf_op jit(solution)/shard_map/while/body/eval_jaxpr/all_gather | solution.py:122
  291.3 122.9 %all-reduce.2.cloned.1.call-start = ((), (), s32[]{:S(2)}) async-start(), calls=%async_computation.3 | async-start | bytes 2097152 | tf_op jit(solution)/shard_map/while/body/eval_jaxpr/psum | solution.py:18
  323.6 90.9 %collective-permute-start = (bf16[128,4096]{1,0:T(8,128)(2,1)S(1)}, bf16[128,4096]{1,0:T(8,128)(2,1)}, u32[]{:S(2)}, u32[]{:S(2)}) collective-permute-start(bf16[128,4096]{1,0:T(8,128)(2,1)S(1)} %copy-done), channel_id=1, source_target_pairs={{0,16},{16,32},{32,48},{48,64},{64,80},{80,96},{96,112},{1,17},{17... | collective-permute-start | bytes 3145736 | tf_op jit(solution)/shard_map/while/body/eval_jaxpr/ppermute | solution.py:13
  330.5 84.1 %copy-start.5 = (f32[4096]{0:T(1024)S(1)}, f32[4096]{0:T(1024)}, u32[]{:S(2)}) copy-start(f32[4096]{0:T(1024)} %get-tuple-element.671) | copy-start | bytes 49156 | tf_op jit(solution)/shard_map/while
  330.5 84.1 %copy-start.8 = (f32[1,4]{1,0:T(1,128)S(1)}, f32[1,4]{1,0:T(1,128)}, u32[]{:S(2)}) copy-start(f32[1,4]{1,0:T(1,128)} %get-tuple-element.697) | copy-start | bytes 52 | tf_op jit(solution)/shard_map/while
  414.6 75.5 %reduce-scatter.2.cloned.1.call-start = ((), (), s32[]{:S(2)}) async-start(), calls=%async_computation.1 | async-start | bytes 1114112 | tf_op jit(solution)/shard_map/while/body/eval_jaxpr/reduce_scatter | solution.py:89
  429.6 92.7 %all-gather.2.cloned.1.call-start = ((), (), s32[]{:S(2)}) async-start(), calls=%async_computation.2 | async-start | bytes 1114112 | tf_op jit(solution)/shard_map/while/body/eval_jaxpr/all_gather | solution.py:122
  491.6 123.1 %all-reduce.2.cloned.1.call-start = ((), (), s32[]{:S(2)}) async-start(), calls=%async_computation.3 | async-start | bytes 2097152 | tf_op jit(solution)/shard_map/while/body/eval_jaxpr/psum | solution.py:18
  524.0 92.2 %collective-permute-start = (bf16[128,4096]{1,0:T(8,128)(2,1)S(1)}, bf16[128,4096]{1,0:T(8,128)(2,1)}, u32[]{:S(2)}, u32[]{:S(2)}) collective-permute-start(bf16[128,4096]{1,0:T(8,128)(2,1)S(1)} %copy-done), channel_id=1, source_target_pairs={{0,16},{16,32},{32,48},{48,64},{64,80},{80,96},{96,112},{1,17},{17... | collective-permute-start | bytes 3145736 | tf_op jit(solution)/shard_map/while/body/eval_jaxpr/ppermute | solution.py:13
  530.8 85.4 %copy-start.5 = (f32[4096]{0:T(1024)S(1)}, f32[4096]{0:T(1024)}, u32[]{:S(2)}) copy-start(f32[4096]{0:T(1024)} %get-tuple-element.671) | copy-start | bytes 49156 | tf_op jit(solution)/shard_map/while
  530.8 85.4 %copy-start.8 = (f32[1,4]{1,0:T(1,128)S(1)}, f32[1,4]{1,0:T(1,128)}, u32[]{:S(2)}) copy-start(f32[1,4]{1,0:T(1,128)} %get-tuple-element.697) | copy-start | bytes 52 | tf_op jit(solution)/shard_map/while
  616.2 75.5 %reduce-scatter.2.cloned.1.call-start = ((), (), s32[]{:S(2)}) async-start(), calls=%async_computation.1 | async-start | bytes 1114112 | tf_op jit(solution)/shard_map/while/body/eval_jaxpr/reduce_scatter | solution.py:89
  631.2 92.8 %all-gather.2.cloned.1.call-start = ((), (), s32[]{:S(2)}) async-start(), calls=%async_computation.2 | async-start | bytes 1114112 | tf_op jit(solution)/shard_map/while/body/eval_jaxpr/all_gather | solution.py:122
  693.2 123.0 %all-reduce.2.cloned.1.call-start = ((), (), s32[]{:S(2)}) async-start(), calls=%async_computation.3 | async-start | bytes 2097152 | tf_op jit(solution)/shard_map/while/body/eval_jaxpr/psum | solution.py:18
  725.7 92.2 %collective-permute-start = (bf16[128,4096]{1,0:T(8,128)(2,1)S(1)}, bf16[128,4096]{1,0:T(8,128)(2,1)}, u32[]{:S(2)}, u32[]{:S(2)}) collective-permute-start(bf16[128,4096]{1,0:T(8,128)(2,1)S(1)} %copy-done), channel_id=1, source_target_pairs={{0,16},{16,32},{32,48},{48,64},{64,80},{80,96},{96,112},{1,17},{17... | collective-permute-start | bytes 3145736 | tf_op jit(solution)/shard_map/while/body/eval_jaxpr/ppermute | solution.py:13
  732.5 85.3 %copy-start.5 = (f32[4096]{0:T(1024)S(1)}, f32[4096]{0:T(1024)}, u32[]{:S(2)}) copy-start(f32[4096]{0:T(1024)} %get-tuple-element.671) | copy-start | bytes 49156 | tf_op jit(solution)/shard_map/while
  732.5 85.3 %copy-start.8 = (f32[1,4]{1,0:T(1,128)S(1)}, f32[1,4]{1,0:T(1,128)}, u32[]{:S(2)}) copy-start(f32[1,4]{1,0:T(1,128)} %get-tuple-element.697) | copy-start | bytes 52 | tf_op jit(solution)/shard_map/while
  817.9 75.5 %reduce-scatter.2.cloned.1.call-start = ((), (), s32[]{:S(2)}) async-start(), calls=%async_computation.1 | async-start | bytes 1114112 | tf_op jit(solution)/shard_map/while/body/eval_jaxpr/reduce_scatter | solution.py:89
  832.9 92.5 %all-gather.2.cloned.1.call-start = ((), (), s32[]{:S(2)}) async-start(), calls=%async_computation.2 | async-start | bytes 1114112 | tf_op jit(solution)/shard_map/while/body/eval_jaxpr/all_gather | solution.py:122
  894.8 122.8 %all-reduce.2.cloned.1.call-start = ((), (), s32[]{:S(2)}) async-start(), calls=%async_computation.3 | async-start | bytes 2097152 | tf_op jit(solution)/shard_map/while/body/eval_jaxpr/psum | solution.py:18
  927.0 90.9 %collective-permute-start = (bf16[128,4096]{1,0:T(8,128)(2,1)S(1)}, bf16[128,4096]{1,0:T(8,128)(2,1)}, u32[]{:S(2)}, u32[]{:S(2)}) collective-permute-start(bf16[128,4096]{1,0:T(8,128)(2,1)S(1)} %copy-done), channel_id=1, source_target_pairs={{0,16},{16,32},{32,48},{48,64},{64,80},{80,96},{96,112},{1,17},{17... | collective-permute-start | bytes 3145736 | tf_op jit(solution)/shard_map/while/body/eval_jaxpr/ppermute | solution.py:13
  1018.0 75.5 %reduce-scatter.2.cloned.1.call-start = ((), (), s32[]{:S(2)}) async-start(), calls=%async_computation.1 | async-start | bytes 1114112 | tf_op jit(solution)/shard_map/while/body/eval_jaxpr/reduce_scatter | solution.py:89
  1033.0 92.7 %all-gather.2.cloned.1.call-start = ((), (), s32[]{:S(2)}) async-start(), calls=%async_computation.2 | async-start | bytes 1114112 | tf_op jit(solution)/shard_map/while/body/eval_jaxpr/all_gather | solution.py:122
  1094.9 122.9 %all-reduce.2.cloned.1.call-start = ((), (), s32[]{:S(2)}) async-start(), calls=%async_computation.3 | async-start | bytes 2097152 | tf_op jit(solution)/shard_map/while/body/eval_jaxpr/psum | solution.py:18
  1127.3 90.9 %collective-permute-start = (bf16[128,4096]{1,0:T(8,128)(2,1)S(1)}, bf16[128,4096]{1,0:T(8,128)(2,1)}, u32[]{:S(2)}, u32[]{:S(2)}) collective-permute-start(bf16[128,4096]{1,0:T(8,128)(2,1)S(1)} %copy-done), channel_id=1, source_target_pairs={{0,16},{16,32},{32,48},{48,64},{64,80},{80,96},{96,112},{1,17},{17... | collective-permute-start | bytes 3145736 | tf_op jit(solution)/shard_map/while/body/eval_jaxpr/ppermute | solution.py:13
  1134.1 84.1 %copy-start.8 = (f32[1,4]{1,0:T(1,128)S(1)}, f32[1,4]{1,0:T(1,128)}, u32[]{:S(2)}) copy-start(f32[1,4]{1,0:T(1,128)} %get-tuple-element.697) | copy-start | bytes 52 | tf_op jit(solution)/shard_map/while
  1218.3 75.5 %reduce-scatter.2.cloned.1.call-start = ((), (), s32[]{:S(2)}) async-start(), calls=%async_computation.1 | async-start | bytes 1114112 | tf_op jit(solution)/shard_map/while/body/eval_jaxpr/reduce_scatter | solution.py:89
  1233.3 92.7 %all-gather.2.cloned.1.call-start = ((), (), s32[]{:S(2)}) async-start(), calls=%async_computation.2 | async-start | bytes 1114112 | tf_op jit(solution)/shard_map/while/body/eval_jaxpr/all_gather | solution.py:122
  1295.2 123.0 %all-reduce.2.cloned.1.call-start = ((), (), s32[]{:S(2)}) async-start(), calls=%async_computation.3 | async-start | bytes 2097152 | tf_op jit(solution)/shard_map/while/body/eval_jaxpr/psum | solution.py:18
  1327.6 91.0 %collective-permute-start = (bf16[128,4096]{1,0:T(8,128)(2,1)S(1)}, bf16[128,4096]{1,0:T(8,128)(2,1)}, u32[]{:S(2)}, u32[]{:S(2)}) collective-permute-start(bf16[128,4096]{1,0:T(8,128)(2,1)S(1)} %copy-done), channel_id=1, source_target_pairs={{0,16},{16,32},{32,48},{48,64},{64,80},{80,96},{96,112},{1,17},{17... | collective-permute-start | bytes 3145736 | tf_op jit(solution)/shard_map/while/body/eval_jaxpr/ppermute | solution.py:13
  1334.4 84.1 %copy-start.5 = (f32[4096]{0:T(1024)S(1)}, f32[4096]{0:T(1024)}, u32[]{:S(2)}) copy-start(f32[4096]{0:T(1024)} %get-tuple-element.671) | copy-start | bytes 49156 | tf_op jit(solution)/shard_map/while
  1334.4 84.1 %copy-start.8 = (f32[1,4]{1,0:T(1,128)S(1)}, f32[1,4]{1,0:T(1,128)}, u32[]{:S(2)}) copy-start(f32[1,4]{1,0:T(1,128)} %get-tuple-element.697) | copy-start | bytes 52 | tf_op jit(solution)/shard_map/while
  1418.6 75.3 %reduce-scatter.2.cloned.1.call-start = ((), (), s32[]{:S(2)}) async-start(), calls=%async_computation.1 | async-start | bytes 1114112 | tf_op jit(solution)/shard_map/while/body/eval_jaxpr/reduce_scatter | solution.py:89
  1433.6 92.8 %all-gather.2.cloned.1.call-start = ((), (), s32[]{:S(2)}) async-start(), calls=%async_computation.2 | async-start | bytes 1114112 | tf_op jit(solution)/shard_map/while/body/eval_jaxpr/all_gather | solution.py:122
  1495.4 123.2 %all-reduce.2.cloned.1.call-start = ((), (), s32[]{:S(2)}) async-start(), calls=%async_computation.3 | async-start | bytes 2097152 | tf_op jit(solution)/shard_map/while/body/eval_jaxpr/psum | solution.py:18
  1528.0 90.9 %collective-permute-start = (bf16[128,4096]{1,0:T(8,128)(2,1)S(1)}, bf16[128,4096]{1,0:T(8,128)(2,1)}, u32[]{:S(2)}, u32[]{:S(2)}) collective-permute-start(bf16[128,4096]{1,0:T(8,128)(2,1)S(1)} %copy-done), channel_id=1, source_target_pairs={{0,16},{16,32},{32,48},{48,64},{64,80},{80,96},{96,112},{1,17},{17... | collective-permute-start | bytes 3145736 | tf_op jit(solution)/shard_map/while/body/eval_jaxpr/ppermute | solution.py:13
  1534.8 84.1 %copy-start.8 = (f32[1,4]{1,0:T(1,128)S(1)}, f32[1,4]{1,0:T(1,128)}, u32[]{:S(2)}) copy-start(f32[1,4]{1,0:T(1,128)} %get-tuple-element.697) | copy-start | bytes 52 | tf_op jit(solution)/shard_map/while
  1619.0 75.5 %reduce-scatter.2.cloned.1.call-start = ((), (), s32[]{:S(2)}) async-start(), calls=%async_computation.1 | async-start | bytes 1114112 | tf_op jit(solution)/shard_map/while/body/eval_jaxpr/reduce_scatter | solution.py:89
  1634.0 92.6 %all-gather.2.cloned.1.call-start = ((), (), s32[]{:S(2)}) async-start(), calls=%async_computation.2 | async-start | bytes 1114112 | tf_op jit(solution)/shard_map/while/body/eval_jaxpr/all_gather | solution.py:122
  1696.0 122.8 %all-reduce.2.cloned.1.call-start = ((), (), s32[]{:S(2)}) async-start(), calls=%async_computation.3 | async-start | bytes 2097152 | tf_op jit(solution)/shard_map/while/body/eval_jaxpr/psum | solution.py:18
  1728.2 90.9 %collective-permute-start = (bf16[128,4096]{1,0:T(8,128)(2,1)S(1)}, bf16[128,4096]{1,0:T(8,128)(2,1)}, u32[]{:S(2)}, u32[]{:S(2)}) collective-permute-start(bf16[128,4096]{1,0:T(8,128)(2,1)S(1)} %copy-done), channel_id=1, source_target_pairs={{0,16},{16,32},{32,48},{48,64},{64,80},{80,96},{96,112},{1,17},{17... | collective-permute-start | bytes 3145736 | tf_op jit(solution)/shard_map/while/body/eval_jaxpr/ppermute | solution.py:13
  (45 other events, 579.7 us)
Sparse Core Ops, SparseCore 0:
  24.6 65.0 reduce-scatter.1
  91.3 30.3 all-gather.1
  124.2 89.7 all-reduce.1
  229.6 60.1 reduce-scatter.1
  291.4 30.5 all-gather.1
  324.3 89.8 all-reduce.1
  429.7 60.2 reduce-scatter.1
  491.8 30.5 all-gather.1
  524.9 89.7 all-reduce.1
  631.3 60.3 reduce-scatter.1
  693.4 30.5 all-gather.1
  726.4 89.8 all-reduce.1
  833.0 60.2 reduce-scatter.1
  895.0 30.4 all-gather.1
  927.8 89.7 all-reduce.1
  1033.1 60.2 reduce-scatter.1
  1095.1 30.5 all-gather.1
  1128.0 89.8 all-reduce.1
  1233.4 60.2 reduce-scatter.1
  1295.4 30.5 all-gather.1
  1328.5 89.7 all-reduce.1
  1433.7 60.1 reduce-scatter.1
  1495.6 30.6 all-gather.1
  1528.7 89.8 all-reduce.1
  1634.1 60.3 reduce-scatter.1
  1696.1 30.4 all-gather.1
  1728.9 89.7 all-reduce.1
where the time goes:
time: 1830 us
  waiting for transfers between devices  1580 us (86%)
  other arithmetic  91.7 us (5%)
  matrix products  74.8 us (4%)
  starting transfers between devices  41 us (2%)
  local copies, waits for them, and re-layouts  25.1 us (1%)
    psum x9, waiting for transfers between devices, broadcast(): return lax.psum(kept, axis)  754 us
    reduce_scatter x9, waiting for transfers between devices, layer(): lax.psum_scatter(jnp.dot(blended_payloads, w_output, preferred_element_ty...  548 us
    all_gather x9, waiting for transfers between devices, advance(): outgoing = lax.all_gather(share, 'seq', axis=0, tiled=True)  276 us
    ppermute x9, starting transfers between devices, from_behind(): return lax.ppermute(x, axis, pairs)  39.8 us
  transfers between devices with their start and end apart: 36, of which 27 were waited for; matrix products, arithmetic and copies ran while one was open for 1% of the time, Pallas kernels for 0%

commit v1 on v0

--- a/solution.py
+++ b/solution.py
@@ -15,7 +15,7 @@
 
 def broadcast(value, axis, source):
     kept = jnp.where(lax.axis_index(axis) == source, value, 0).astype(value.dtype)
-    return lax.psum(kept, axis)
+    return jnp.sum(lax.all_gather(kept, axis), axis=0)
 
 
 def normalize(row_block, gain_vector):

time: 1830 us -> 2130 us (1.16)
  waiting for transfers between devices: 1580 us -> 1830 us
  other arithmetic: 91.7 us -> 140 us
    all_gather x0 -> x9, waiting for transfers between devices: none -> 1010 us  [broadcast(): return jnp.sum(lax.all_gather(kept, axis), axis=0)]
    psum x9 -> x0, waiting for transfers between devices: 754 us -> none  [broadcast(): return lax.psum(kept, axis)]
    reduce_sum x0 -> x9, other arithmetic: none -> 44.1 us  [broadcast(): return jnp.sum(lax.all_gather(kept, axis), axis=0)]
  transfers between devices with their start and end apart: 36 -> 36, of which waited for: 27 -> 27; matrix products, arithmetic and copies ran while one was open for 1% -> 3% of each run, Pallas kernels for 0% -> 0%
where the time goes in v1:
time: 2130 us
  waiting for transfers between devices  1830 us (86%)
  other arithmetic  140 us (7%)
  matrix products  74.7 us (4%)
  starting transfers between devices  40.8 us (2%)
    all_gather x9, waiting for transfers between devices, broadcast(): return jnp.sum(lax.all_gather(kept, axis), axis=0)  1010 us
    reduce_scatter x9, waiting for transfers between devices, layer(): lax.psum_scatter(jnp.dot(blended_payloads, w_output, preferred_element_ty...  546 us
    all_gather x9, waiting for transfers between devices, advance(): outgoing = lax.all_gather(share, 'seq', axis=0, tiled=True)  277 us
    reduce_sum x9, other arithmetic, broadcast(): return jnp.sum(lax.all_gather(kept, axis), axis=0)  44.1 us
  transfers between devices with their start and end apart: 36, of which 27 were waited for; matrix products, arithmetic and copies ran while one was open for 3% of the time, Pallas kernels for 0%

profile of v1, /device:TPU:0, one launch (start us, length us, event | category | flops | bytes accessed | tf_op | source)
XLA Modules:
  0.0 2125.8 jit_solution(2730629486686893138)
XLA Ops:
  9.5 2109.5 %while.20 = (s32[]{:T(128)}, bf16[128,4096]{1,0:T(8,128)(2,1)}, bf16[2,128,4096]{2,1,0:T(8,128)(2,1)S(1)}, bf16[2,128,4096]{2,1,0:T(8,128)(2,1)}, pred[]{:T(512)...) while((s32[]{:T(128)}, bf16[128,4096]{1,0:T(8,128)(2,1)}, ...), condition=%wide.region_8.9_spmd, body=%wide.region_0.8_spmd.sunk | while | flops 1107953536 | bytes 104928584 | solution.py:135
  24.7 65.0 %reduce-scatter.2.cloned.1.call-done = bf16[8,4096]{1,0:T(8,128)(2,1)} async-done(((bf16[128,4096]{1,0:T(8,128)(2,1)}), bf16[8,4096]{1,0:T(8,128)(2,1)}) %reduce-scatter.2.cloned.1.call-update) | async-done | bytes 65552 | tf_op jit(solution)/shard_map/while/body/eval_jaxpr/reduce_scatter | solution.py:89
  91.3 30.7 %all-gather.6.cloned.1.call-done = bf16[128,4096]{1,0:T(8,128)(2,1)} async-done(((bf16[8,4096]{1,0:T(8,128)(2,1)}), bf16[128,4096]{1,0:T(8,128)(2,1)}) %all-gather.6.cloned.1.call-update) | async-done | bytes 1048592 | tf_op jit(solution)/shard_map/while/body/eval_jaxpr/all_gather | solution.py:122
  123.0 4.4 collective-permute-start
  130.2 112.4 %all-gather.8.cloned.1.call-done = bf16[1024,4096]{1,0:T(8,128)(2,1)} async-done(((bf16[128,4096]{1,0:T(8,128)(2,1)}), bf16[1024,4096]{1,0:T(8,128)(2,1)}) %all-gather.8.cloned.1.call-update) | async-done | bytes 8388624 | tf_op jit(solution)/shard_map/while/body/eval_jaxpr/all_gather | solution.py:18
  242.6 4.9 reduce_sum.110
  263.4 60.1 %reduce-scatter.2.cloned.1.call-done = bf16[8,4096]{1,0:T(8,128)(2,1)} async-done(((bf16[128,4096]{1,0:T(8,128)(2,1)}), bf16[8,4096]{1,0:T(8,128)(2,1)}) %reduce-scatter.2.cloned.1.call-update) | async-done | bytes 65552 | tf_op jit(solution)/shard_map/while/body/eval_jaxpr/reduce_scatter | solution.py:89
  325.0 30.8 %all-gather.6.cloned.1.call-done = bf16[128,4096]{1,0:T(8,128)(2,1)} async-done(((bf16[8,4096]{1,0:T(8,128)(2,1)}), bf16[128,4096]{1,0:T(8,128)(2,1)}) %all-gather.6.cloned.1.call-update) | async-done | bytes 1048592 | tf_op jit(solution)/shard_map/while/body/eval_jaxpr/all_gather | solution.py:122
  356.9 4.4 collective-permute-start
  364.1 112.2 %all-gather.8.cloned.1.call-done = bf16[1024,4096]{1,0:T(8,128)(2,1)} async-done(((bf16[128,4096]{1,0:T(8,128)(2,1)}), bf16[1024,4096]{1,0:T(8,128)(2,1)}) %all-gather.8.cloned.1.call-update) | async-done | bytes 8388624 | tf_op jit(solution)/shard_map/while/body/eval_jaxpr/all_gather | solution.py:18
  476.3 4.9 reduce_sum.110
  494.0 3.1 convolution_convert_fusion.8
  497.1 60.2 %reduce-scatter.2.cloned.1.call-done = bf16[8,4096]{1,0:T(8,128)(2,1)} async-done(((bf16[128,4096]{1,0:T(8,128)(2,1)}), bf16[8,4096]{1,0:T(8,128)(2,1)}) %reduce-scatter.2.cloned.1.call-update) | async-done | bytes 65552 | tf_op jit(solution)/shard_map/while/body/eval_jaxpr/reduce_scatter | solution.py:89
  558.9 30.8 %all-gather.6.cloned.1.call-done = bf16[128,4096]{1,0:T(8,128)(2,1)} async-done(((bf16[8,4096]{1,0:T(8,128)(2,1)}), bf16[128,4096]{1,0:T(8,128)(2,1)}) %all-gather.6.cloned.1.call-update) | async-done | bytes 1048592 | tf_op jit(solution)/shard_map/while/body/eval_jaxpr/all_gather | solution.py:122
  590.8 4.4 collective-permute-start
  598.0 112.4 %all-gather.8.cloned.1.call-done = bf16[1024,4096]{1,0:T(8,128)(2,1)} async-done(((bf16[128,4096]{1,0:T(8,128)(2,1)}), bf16[1024,4096]{1,0:T(8,128)(2,1)}) %all-gather.8.cloned.1.call-update) | async-done | bytes 8388624 | tf_op jit(solution)/shard_map/while/body/eval_jaxpr/all_gather | solution.py:18
  710.4 4.9 reduce_sum.110
  731.2 60.2 %reduce-scatter.2.cloned.1.call-done = bf16[8,4096]{1,0:T(8,128)(2,1)} async-done(((bf16[128,4096]{1,0:T(8,128)(2,1)}), bf16[8,4096]{1,0:T(8,128)(2,1)}) %reduce-scatter.2.cloned.1.call-update) | async-done | bytes 65552 | tf_op jit(solution)/shard_map/while/body/eval_jaxpr/reduce_scatter | solution.py:89
  792.9 30.9 %all-gather.6.cloned.1.call-done = bf16[128,4096]{1,0:T(8,128)(2,1)} async-done(((bf16[8,4096]{1,0:T(8,128)(2,1)}), bf16[128,4096]{1,0:T(8,128)(2,1)}) %all-gather.6.cloned.1.call-update) | async-done | bytes 1048592 | tf_op jit(solution)/shard_map/while/body/eval_jaxpr/all_gather | solution.py:122
  824.8 4.4 collective-permute-start
  832.0 112.2 %all-gather.8.cloned.1.call-done = bf16[1024,4096]{1,0:T(8,128)(2,1)} async-done(((bf16[128,4096]{1,0:T(8,128)(2,1)}), bf16[1024,4096]{1,0:T(8,128)(2,1)}) %all-gather.8.cloned.1.call-update) | async-done | bytes 8388624 | tf_op jit(solution)/shard_map/while/body/eval_jaxpr/all_gather | solution.py:18
  944.3 4.9 reduce_sum.110
  962.0 3.1 convolution_convert_fusion.8
  965.1 60.2 %reduce-scatter.2.cloned.1.call-done = bf16[8,4096]{1,0:T(8,128)(2,1)} async-done(((bf16[128,4096]{1,0:T(8,128)(2,1)}), bf16[8,4096]{1,0:T(8,128)(2,1)}) %reduce-scatter.2.cloned.1.call-update) | async-done | bytes 65552 | tf_op jit(solution)/shard_map/while/body/eval_jaxpr/reduce_scatter | solution.py:89
  1026.9 30.7 %all-gather.6.cloned.1.call-done = bf16[128,4096]{1,0:T(8,128)(2,1)} async-done(((bf16[8,4096]{1,0:T(8,128)(2,1)}), bf16[128,4096]{1,0:T(8,128)(2,1)}) %all-gather.6.cloned.1.call-update) | async-done | bytes 1048592 | tf_op jit(solution)/shard_map/while/body/eval_jaxpr/all_gather | solution.py:122
  1058.7 4.4 collective-permute-start
  1065.9 112.2 %all-gather.8.cloned.1.call-done = bf16[1024,4096]{1,0:T(8,128)(2,1)} async-done(((bf16[128,4096]{1,0:T(8,128)(2,1)}), bf16[1024,4096]{1,0:T(8,128)(2,1)}) %all-gather.8.cloned.1.call-update) | async-done | bytes 8388624 | tf_op jit(solution)/shard_map/while/body/eval_jaxpr/all_gather | solution.py:18
  1178.1 4.9 reduce_sum.110
  1198.9 60.2 %reduce-scatter.2.cloned.1.call-done = bf16[8,4096]{1,0:T(8,128)(2,1)} async-done(((bf16[128,4096]{1,0:T(8,128)(2,1)}), bf16[8,4096]{1,0:T(8,128)(2,1)}) %reduce-scatter.2.cloned.1.call-update) | async-done | bytes 65552 | tf_op jit(solution)/shard_map/while/body/eval_jaxpr/reduce_scatter | solution.py:89
  1260.6 30.8 %all-gather.6.cloned.1.call-done = bf16[128,4096]{1,0:T(8,128)(2,1)} async-done(((bf16[8,4096]{1,0:T(8,128)(2,1)}), bf16[128,4096]{1,0:T(8,128)(2,1)}) %all-gather.6.cloned.1.call-update) | async-done | bytes 1048592 | tf_op jit(solution)/shard_map/while/body/eval_jaxpr/all_gather | solution.py:122
  1292.5 4.4 collective-permute-start
  1299.7 112.2 %all-gather.8.cloned.1.call-done = bf16[1024,4096]{1,0:T(8,128)(2,1)} async-done(((bf16[128,4096]{1,0:T(8,128)(2,1)}), bf16[1024,4096]{1,0:T(8,128)(2,1)}) %all-gather.8.cloned.1.call-update) | async-done | bytes 8388624 | tf_op jit(solution)/shard_map/while/body/eval_jaxpr/all_gather | solution.py:18
  1411.9 4.9 reduce_sum.110
  1432.7 60.1 %reduce-scatter.2.cloned.1.call-done = bf16[8,4096]{1,0:T(8,128)(2,1)} async-done(((bf16[128,4096]{1,0:T(8,128)(2,1)}), bf16[8,4096]{1,0:T(8,128)(2,1)}) %reduce-scatter.2.cloned.1.call-update) | async-done | bytes 65552 | tf_op jit(solution)/shard_map/while/body/eval_jaxpr/reduce_scatter | solution.py:89
  1494.3 30.8 %all-gather.6.cloned.1.call-done = bf16[128,4096]{1,0:T(8,128)(2,1)} async-done(((bf16[8,4096]{1,0:T(8,128)(2,1)}), bf16[128,4096]{1,0:T(8,128)(2,1)}) %all-gather.6.cloned.1.call-update) | async-done | bytes 1048592 | tf_op jit(solution)/shard_map/while/body/eval_jaxpr/all_gather | solution.py:122
  1526.2 4.4 collective-permute-start
  1533.4 112.4 %all-gather.8.cloned.1.call-done = bf16[1024,4096]{1,0:T(8,128)(2,1)} async-done(((bf16[128,4096]{1,0:T(8,128)(2,1)}), bf16[1024,4096]{1,0:T(8,128)(2,1)}) %all-gather.8.cloned.1.call-update) | async-done | bytes 8388624 | tf_op jit(solution)/shard_map/while/body/eval_jaxpr/all_gather | solution.py:18
  1645.7 4.9 reduce_sum.110
  1666.5 60.3 %reduce-scatter.2.cloned.1.call-done = bf16[8,4096]{1,0:T(8,128)(2,1)} async-done(((bf16[128,4096]{1,0:T(8,128)(2,1)}), bf16[8,4096]{1,0:T(8,128)(2,1)}) %reduce-scatter.2.cloned.1.call-update) | async-done | bytes 65552 | tf_op jit(solution)/shard_map/while/body/eval_jaxpr/reduce_scatter | solution.py:89
  1728.4 30.8 %all-gather.6.cloned.1.call-done = bf16[128,4096]{1,0:T(8,128)(2,1)} async-done(((bf16[8,4096]{1,0:T(8,128)(2,1)}), bf16[128,4096]{1,0:T(8,128)(2,1)}) %all-gather.6.cloned.1.call-update) | async-done | bytes 1048592 | tf_op jit(solution)/shard_map/while/body/eval_jaxpr/all_gather | solution.py:122
  1760.2 4.4 collective-permute-start
  1767.4 112.2 %all-gather.8.cloned.1.call-done = bf16[1024,4096]{1,0:T(8,128)(2,1)} async-done(((bf16[128,4096]{1,0:T(8,128)(2,1)}), bf16[1024,4096]{1,0:T(8,128)(2,1)}) %all-gather.8.cloned.1.call-update) | async-done | bytes 8388624 | tf_op jit(solution)/shard_map/while/body/eval_jaxpr/all_gather | solution.py:18
  1879.7 4.9 reduce_sum.110
  1900.5 60.1 %reduce-scatter.2.cloned.1.call-done = bf16[8,4096]{1,0:T(8,128)(2,1)} async-done(((bf16[128,4096]{1,0:T(8,128)(2,1)}), bf16[8,4096]{1,0:T(8,128)(2,1)}) %reduce-scatter.2.cloned.1.call-update) | async-done | bytes 65552 | tf_op jit(solution)/shard_map/while/body/eval_jaxpr/reduce_scatter | solution.py:89
  1962.1 30.7 %all-gather.6.cloned.1.call-done = bf16[128,4096]{1,0:T(8,128)(2,1)} async-done(((bf16[8,4096]{1,0:T(8,128)(2,1)}), bf16[128,4096]{1,0:T(8,128)(2,1)}) %all-gather.6.cloned.1.call-update) | async-done | bytes 1048592 | tf_op jit(solution)/shard_map/while/body/eval_jaxpr/all_gather | solution.py:122
  1993.9 4.4 collective-permute-start
  2001.1 112.2 %all-gather.8.cloned.1.call-done = bf16[1024,4096]{1,0:T(8,128)(2,1)} async-done(((bf16[128,4096]{1,0:T(8,128)(2,1)}), bf16[1024,4096]{1,0:T(8,128)(2,1)}) %all-gather.8.cloned.1.call-update) | async-done | bytes 8388624 | tf_op jit(solution)/shard_map/while/body/eval_jaxpr/all_gather | solution.py:18
  2113.3 4.9 reduce_sum.110
  (322 shorter events, 186.7 us)
Async XLA Ops:
  6.8 2.7 copy-start.2
  6.8 2.7 copy-start.3
  6.8 2.7 copy-start.6
  9.5 80.2 %reduce-scatter.2.cloned.1.call-start = ((), (), s32[]{:S(2)}) async-start(), calls=%async_computation.1 | async-start | bytes 1114112 | tf_op jit(solution)/shard_map/while/body/eval_jaxpr/reduce_scatter | solution.py:89
  14.8 3.4 copy-start
  24.6 97.3 %all-gather.6.cloned.1.call-start = ((), (), s32[]{:S(2)}) async-start(), calls=%async_computation.2 | async-start | bytes 1114112 | tf_op jit(solution)/shard_map/while/body/eval_jaxpr/all_gather | solution.py:122
  91.2 151.4 %all-gather.8.cloned.1.call-start = ((), (), s32[]{:S(2)}) async-start(), calls=%async_computation.3 | async-start | bytes 9437184 | tf_op jit(solution)/shard_map/while/body/eval_jaxpr/all_gather | solution.py:18
  123.0 124.9 %collective-permute-start = (bf16[128,4096]{1,0:T(8,128)(2,1)}, bf16[128,4096]{1,0:T(8,128)(2,1)}, u32[]{:S(2)}, u32[]{:S(2)}) collective-permute-start(bf16[128,4096]{1,0:T(8,128)(2,1)} %all-gather.6.cloned.1.call-done), channel_id=1, source_target_pairs={{0,16},{16,32},{32,48},{48,64},{64,80},{80,96},{96,112},{1,17},{17... | collective-permute-start | bytes 3145736 | tf_op jit(solution)/shard_map/while/body/eval_jaxpr/ppermute | solution.py:13
  248.2 75.2 %reduce-scatter.2.cloned.1.call-start = ((), (), s32[]{:S(2)}) async-start(), calls=%async_computation.1 | async-start | bytes 1114112 | tf_op jit(solution)/shard_map/while/body/eval_jaxpr/reduce_scatter | solution.py:89
  253.5 3.4 copy-start
  263.3 92.4 %all-gather.6.cloned.1.call-start = ((), (), s32[]{:S(2)}) async-start(), calls=%async_computation.2 | async-start | bytes 1114112 | tf_op jit(solution)/shard_map/while/body/eval_jaxpr/all_gather | solution.py:122
  325.0 151.3 %all-gather.8.cloned.1.call-start = ((), (), s32[]{:S(2)}) async-start(), calls=%async_computation.3 | async-start | bytes 9437184 | tf_op jit(solution)/shard_map/while/body/eval_jaxpr/all_gather | solution.py:18
  356.9 124.7 %collective-permute-start = (bf16[128,4096]{1,0:T(8,128)(2,1)}, bf16[128,4096]{1,0:T(8,128)(2,1)}, u32[]{:S(2)}, u32[]{:S(2)}) collective-permute-start(bf16[128,4096]{1,0:T(8,128)(2,1)} %all-gather.6.cloned.1.call-done), channel_id=1, source_target_pairs={{0,16},{16,32},{32,48},{48,64},{64,80},{80,96},{96,112},{1,17},{17... | collective-permute-start | bytes 3145736 | tf_op jit(solution)/shard_map/while/body/eval_jaxpr/ppermute | solution.py:13
  481.9 75.4 %reduce-scatter.2.cloned.1.call-start = ((), (), s32[]{:S(2)}) async-start(), calls=%async_computation.1 | async-start | bytes 1114112 | tf_op jit(solution)/shard_map/while/body/eval_jaxpr/reduce_scatter | solution.py:89
  487.2 3.4 copy-start
  497.0 92.7 %all-gather.6.cloned.1.call-start = ((), (), s32[]{:S(2)}) async-start(), calls=%async_computation.2 | async-start | bytes 1114112 | tf_op jit(solution)/shard_map/while/body/eval_jaxpr/all_gather | solution.py:122
  558.8 151.6 %all-gather.8.cloned.1.call-start = ((), (), s32[]{:S(2)}) async-start(), calls=%async_computation.3 | async-start | bytes 9437184 | tf_op jit(solution)/shard_map/while/body/eval_jaxpr/all_gather | solution.py:18
  590.8 124.9 %collective-permute-start = (bf16[128,4096]{1,0:T(8,128)(2,1)}, bf16[128,4096]{1,0:T(8,128)(2,1)}, u32[]{:S(2)}, u32[]{:S(2)}) collective-permute-start(bf16[128,4096]{1,0:T(8,128)(2,1)} %all-gather.6.cloned.1.call-done), channel_id=1, source_target_pairs={{0,16},{16,32},{32,48},{48,64},{64,80},{80,96},{96,112},{1,17},{17... | collective-permute-start | bytes 3145736 | tf_op jit(solution)/shard_map/while/body/eval_jaxpr/ppermute | solution.py:13
  716.0 75.3 %reduce-scatter.2.cloned.1.call-start = ((), (), s32[]{:S(2)}) async-start(), calls=%async_computation.1 | async-start | bytes 1114112 | tf_op jit(solution)/shard_map/while/body/eval_jaxpr/reduce_scatter | solution.py:89
  721.3 3.4 copy-start
  731.1 92.6 %all-gather.6.cloned.1.call-start = ((), (), s32[]{:S(2)}) async-start(), calls=%async_computation.2 | async-start | bytes 1114112 | tf_op jit(solution)/shard_map/while/body/eval_jaxpr/all_gather | solution.py:122
  792.8 151.5 %all-gather.8.cloned.1.call-start = ((), (), s32[]{:S(2)}) async-start(), calls=%async_computation.3 | async-start | bytes 9437184 | tf_op jit(solution)/shard_map/while/body/eval_jaxpr/all_gather | solution.py:18
  824.8 124.7 %collective-permute-start = (bf16[128,4096]{1,0:T(8,128)(2,1)}, bf16[128,4096]{1,0:T(8,128)(2,1)}, u32[]{:S(2)}, u32[]{:S(2)}) collective-permute-start(bf16[128,4096]{1,0:T(8,128)(2,1)} %all-gather.6.cloned.1.call-done), channel_id=1, source_target_pairs={{0,16},{16,32},{32,48},{48,64},{64,80},{80,96},{96,112},{1,17},{17... | collective-permute-start | bytes 3145736 | tf_op jit(solution)/shard_map/while/body/eval_jaxpr/ppermute | solution.py:13
  949.9 75.4 %reduce-scatter.2.cloned.1.call-start = ((), (), s32[]{:S(2)}) async-start(), calls=%async_computation.1 | async-start | bytes 1114112 | tf_op jit(solution)/shard_map/while/body/eval_jaxpr/reduce_scatter | solution.py:89
  955.2 3.4 copy-start
  965.0 92.5 %all-gather.6.cloned.1.call-start = ((), (), s32[]{:S(2)}) async-start(), calls=%async_computation.2 | async-start | bytes 1114112 | tf_op jit(solution)/shard_map/while/body/eval_jaxpr/all_gather | solution.py:122
  1026.8 151.3 %all-gather.8.cloned.1.call-start = ((), (), s32[]{:S(2)}) async-start(), calls=%async_computation.3 | async-start | bytes 9437184 | tf_op jit(solution)/shard_map/while/body/eval_jaxpr/all_gather | solution.py:18
  1058.7 124.7 %collective-permute-start = (bf16[128,4096]{1,0:T(8,128)(2,1)}, bf16[128,4096]{1,0:T(8,128)(2,1)}, u32[]{:S(2)}, u32[]{:S(2)}) collective-permute-start(bf16[128,4096]{1,0:T(8,128)(2,1)} %all-gather.6.cloned.1.call-done), channel_id=1, source_target_pairs={{0,16},{16,32},{32,48},{48,64},{64,80},{80,96},{96,112},{1,17},{17... | collective-permute-start | bytes 3145736 | tf_op jit(solution)/shard_map/while/body/eval_jaxpr/ppermute | solution.py:13
  1183.7 75.3 %reduce-scatter.2.cloned.1.call-start = ((), (), s32[]{:S(2)}) async-start(), calls=%async_computation.1 | async-start | bytes 1114112 | tf_op jit(solution)/shard_map/while/body/eval_jaxpr/reduce_scatter | solution.py:89
  1189.0 3.4 copy-start
  1198.8 92.5 %all-gather.6.cloned.1.call-start = ((), (), s32[]{:S(2)}) async-start(), calls=%async_computation.2 | async-start | bytes 1114112 | tf_op jit(solution)/shard_map/while/body/eval_jaxpr/all_gather | solution.py:122
  1260.5 151.4 %all-gather.8.cloned.1.call-start = ((), (), s32[]{:S(2)}) async-start(), calls=%async_computation.3 | async-start | bytes 9437184 | tf_op jit(solution)/shard_map/while/body/eval_jaxpr/all_gather | solution.py:18
  1292.5 124.7 %collective-permute-start = (bf16[128,4096]{1,0:T(8,128)(2,1)}, bf16[128,4096]{1,0:T(8,128)(2,1)}, u32[]{:S(2)}, u32[]{:S(2)}) collective-permute-start(bf16[128,4096]{1,0:T(8,128)(2,1)} %all-gather.6.cloned.1.call-done), channel_id=1, source_target_pairs={{0,16},{16,32},{32,48},{48,64},{64,80},{80,96},{96,112},{1,17},{17... | collective-permute-start | bytes 3145736 | tf_op jit(solution)/shard_map/while/body/eval_jaxpr/ppermute | solution.py:13
  1417.5 75.2 %reduce-scatter.2.cloned.1.call-start = ((), (), s32[]{:S(2)}) async-start(), calls=%async_computation.1 | async-start | bytes 1114112 | tf_op jit(solution)/shard_map/while/body/eval_jaxpr/reduce_scatter | solution.py:89
  1422.8 3.4 copy-start
  1432.6 92.4 %all-gather.6.cloned.1.call-start = ((), (), s32[]{:S(2)}) async-start(), calls=%async_computation.2 | async-start | bytes 1114112 | tf_op jit(solution)/shard_map/while/body/eval_jaxpr/all_gather | solution.py:122
  1494.3 151.5 %all-gather.8.cloned.1.call-start = ((), (), s32[]{:S(2)}) async-start(), calls=%async_computation.3 | async-start | bytes 9437184 | tf_op jit(solution)/shard_map/while/body/eval_jaxpr/all_gather | solution.py:18
  1526.2 124.9 %collective-permute-start = (bf16[128,4096]{1,0:T(8,128)(2,1)}, bf16[128,4096]{1,0:T(8,128)(2,1)}, u32[]{:S(2)}, u32[]{:S(2)}) collective-permute-start(bf16[128,4096]{1,0:T(8,128)(2,1)} %all-gather.6.cloned.1.call-done), channel_id=1, source_target_pairs={{0,16},{16,32},{32,48},{48,64},{64,80},{80,96},{96,112},{1,17},{17... | collective-permute-start | bytes 3145736 | tf_op jit(solution)/shard_map/while/body/eval_jaxpr/ppermute | solution.py:13
  1651.4 75.4 %reduce-scatter.2.cloned.1.call-start = ((), (), s32[]{:S(2)}) async-start(), calls=%async_computation.1 | async-start | bytes 1114112 | tf_op jit(solution)/shard_map/while/body/eval_jaxpr/reduce_scatter | solution.py:89
  1656.6 3.4 copy-start
  1666.5 92.7 %all-gather.6.cloned.1.call-start = ((), (), s32[]{:S(2)}) async-start(), calls=%async_computation.2 | async-start | bytes 1114112 | tf_op jit(solution)/shard_map/while/body/eval_jaxpr/all_gather | solution.py:122
  1728.3 151.4 %all-gather.8.cloned.1.call-start = ((), (), s32[]{:S(2)}) async-start(), calls=%async_computation.3 | async-start | bytes 9437184 | tf_op jit(solution)/shard_map/while/body/eval_jaxpr/all_gather | solution.py:18
  1760.2 124.7 %collective-permute-start = (bf16[128,4096]{1,0:T(8,128)(2,1)}, bf16[128,4096]{1,0:T(8,128)(2,1)}, u32[]{:S(2)}, u32[]{:S(2)}) collective-permute-start(bf16[128,4096]{1,0:T(8,128)(2,1)} %all-gather.6.cloned.1.call-done), channel_id=1, source_target_pairs={{0,16},{16,32},{32,48},{48,64},{64,80},{80,96},{96,112},{1,17},{17... | collective-permute-start | bytes 3145736 | tf_op jit(solution)/shard_map/while/body/eval_jaxpr/ppermute | solution.py:13
  1885.3 75.2 %reduce-scatter.2.cloned.1.call-start = ((), (), s32[]{:S(2)}) async-start(), calls=%async_computation.1 | async-start | bytes 1114112 | tf_op jit(solution)/shard_map/while/body/eval_jaxpr/reduce_scatter | solution.py:89
  1890.6 3.4 copy-start
  1900.4 92.4 %all-gather.6.cloned.1.call-start = ((), (), s32[]{:S(2)}) async-start(), calls=%async_computation.2 | async-start | bytes 1114112 | tf_op jit(solution)/shard_map/while/body/eval_jaxpr/all_gather | solution.py:122
  1962.0 151.3 %all-gather.8.cloned.1.call-start = ((), (), s32[]{:S(2)}) async-start(), calls=%async_computation.3 | async-start | bytes 9437184 | tf_op jit(solution)/shard_map/while/body/eval_jaxpr/all_gather | solution.py:18
  1993.9 124.7 %collective-permute-start = (bf16[128,4096]{1,0:T(8,128)(2,1)}, bf16[128,4096]{1,0:T(8,128)(2,1)}, u32[]{:S(2)}, u32[]{:S(2)}) collective-permute-start(bf16[128,4096]{1,0:T(8,128)(2,1)} %all-gather.6.cloned.1.call-done), channel_id=1, source_target_pairs={{0,16},{16,32},{32,48},{48,64},{64,80},{80,96},{96,112},{1,17},{17... | collective-permute-start | bytes 3145736 | tf_op jit(solution)/shard_map/while/body/eval_jaxpr/ppermute | solution.py:13
  (36 other events, 49.8 us)
Sparse Core Ops, SparseCore 0:
  24.8 64.8 reduce-scatter.1
  91.4 30.4 all-gather.5
  124.3 118.2 all-gather.7
  263.4 59.9 reduce-scatter.1
  325.1 30.6 all-gather.5
  358.0 118.2 all-gather.7
  497.2 60.1 reduce-scatter.1
  559.0 30.6 all-gather.5
  592.1 118.2 all-gather.7
  731.2 60.0 reduce-scatter.1
  793.0 30.6 all-gather.5
  826.0 118.2 all-gather.7
  965.1 60.1 reduce-scatter.1
  1026.9 30.6 all-gather.5
  1059.8 118.2 all-gather.7
  1198.9 60.0 reduce-scatter.1
  1260.7 30.6 all-gather.5
  1293.6 118.2 all-gather.7
  1432.8 59.9 reduce-scatter.1
  1494.4 30.6 all-gather.5
  1527.5 118.2 all-gather.7
  1666.6 60.1 reduce-scatter.1
  1728.5 30.5 all-gather.5
  1761.4 118.2 all-gather.7
  1900.5 59.9 reduce-scatter.1
  1962.2 30.6 all-gather.5
  1995.0 118.2 all-gather.7
